TPU v7x, 128 devices: a whole 4x4x4 slice. The times are simulated.
128 devices in a mesh: rows: 32 (over y, x_hi, z), cols: 4 (over x_lo, core).
Axes of the slice: x: 4 (x_hi: 2, x_lo: 2; x = x_hi * 2 + x_lo), y: 4, z: 4, core: 2. Of those that a mesh axis runs over, the one named last changes fastest.
Arguments:
- tracks: float32 [1024, 2, 65536], P(('rows', 'cols')), may hold values from -200 to 200
- pixel_order: int32 [65536], P('rows'), may hold values from 0 to 65535, as said below
- pairing: int32 [2, 4], replicated, may hold values from 0 to 2
Outputs:
- rotated: float32 [65536, 2048], P('rows', 'cols')
Inputs may be any that keep to these rules, and one draw needn't show every extreme that they name: `pixel_order`: A permutation of 0 to 65535 that maps each aligned block of 2048 rows onto the same block of pixels.
All inputs are finite; a program needn't handle non-finite values.
Results may differ from a plain program's by a relative error of at most 0.0001.
Values sent between devices are 32-bit elements; how exact they have to be, the bound alone decides.
A program may use at most 64 MiB of HBM per device.

v0:
```python
import jax
import jax.numpy as jnp
from jax import lax
from jax.experimental import pallas as pl
from jax.experimental.pallas import tpu as pltpu
from jax.sharding import PartitionSpec as P

F32 = jnp.float32
MESH = pl.DeviceIdType.MESH
ANY = pl.BlockSpec(memory_space=pl.ANY)
SMEM = pl.BlockSpec(memory_space=pltpu.SMEM)
HIGH = lax.Precision.HIGH
NS_STEPS = 6
ROWS = 32
COLS = 4
ALL = ROWS * COLS
PIX = 2048
TILE = 256


def product(a, b):
    return jnp.dot(a, b, precision=HIGH, preferred_element_type=F32)


def product_of_rows(a, b):
    return lax.dot_general(a, b, (((0,), (0,)), ((), ())), precision=HIGH, preferred_element_type=F32)


def shifted(yr, yc, dy, dx, dz, dc):
    y = (yr // 8 + dy) % 4
    x = ((yr // 4 % 2) * 2 + yc // 2 + dx) % 4
    z = (yr % 4 + dz) % 4
    return (y * 2 + x // 2) * 4 + z, (x % 2) * 2 + (yc % 2 + dc) % 2


def any_peer(i, yr, yc):
    first, second, third = i // 2 % 4, i // 8 % 4, i // 32
    return shifted(yr, yc, first + second, first, first + third + 2 * second, i % 2)


def row_peer(i, yr):
    y = (yr // 8 + i // 4 % 4) % 4
    x = (yr // 4 % 2 + i // 16) % 2
    z = (yr % 4 + i % 4) % 4
    return (y * 2 + x) * 4 + z


def roles(choice):
    low = jnp.where(choice == 2, 1, 0)
    high = jnp.where(choice == 0, 1, 2)
    return low, high, 2 - choice


def tile(i):
    return pl.ds(pl.multiple_of(i * TILE, TILE), TILE)


def rotations(couplings, state):
    size = 128
    row = lax.broadcasted_iota(jnp.int32, (size, size), 0)
    col = lax.broadcasted_iota(jnp.int32, (size, size), 1)
    eye = jnp.where(row == col, 1.0, 0.0).astype(F32)
    count = 2 * len(couplings)
    flipped = [c.T for c in couplings]
    for k, c in enumerate(couplings):
        total = 1.0 + jnp.sum(jnp.sum(c * c, axis=1, keepdims=True), axis=0, keepdims=True)
        start = eye * (1.0 / jnp.sqrt(total))
        for m, square in ((2 * k, product(c, flipped[k])), (2 * k + 1, product(flipped[k], c))):
            state[m, :size, :] = (eye + square) / total
            state[m, size:, :] = start

    def step(_, carry):
        held = [state[m] for m in range(count)]
        factors = [1.5 * eye - 0.5 * h[:size] for h in held]
        once = [product(h, f) for h, f in zip(held, factors)]
        twice = [product(o[:size], f) for o, f in zip(once, factors)]
        for m in range(count):
            state[m, :size, :] = twice[m]
            state[m, size:, :] = once[m][size:]
        return carry

    lax.fori_loop(0, NS_STEPS - 1, step, 0)
    last = [product(state[m, size:, :], 1.5 * eye - 0.5 * state[m, :size, :]) for m in range(count)]
    out = []
    for k, c in enumerate(couplings):
        cross = product(last[2 * k], c)
        out.append((last[2 * k], cross, -cross.T, last[2 * k + 1]))
    return out


def steps_kernel(
    v_ref, order_ref, pairing_ref, y_ref, z_ref, qn_ref, turn_ref,
    vv, send, recv, flat, xt, yy, z, q, diag, parts, arrived, own, coup, coupn, rot, state,
    load_sem, out_sem, a2a_send, a2a_recv, rs_send, rs_recv, ag_send, ag_recv, z_send, z_recv, q_send, q_recv,
):
    yr, yc = lax.axis_index("rows"), lax.axis_index("cols")
    me = yr * COLS + yc
    after, before = (yc + 1) % COLS, (yc + COLS - 1) % COLS
    barrier = pltpu.get_barrier_semaphore()

    def load(frame):
        lines = pl.ds(frame * 1024, 1024)
        return pltpu.make_async_copy(v_ref.at[lines], vv.at[lines], load_sem.at[frame])

    for s in range(4):
        load(s).start()
        load(4 + s).start()

    def greet(i, carry):
        pl.semaphore_signal(barrier, inc=1, device_id=any_peer(i, yr, yc), device_id_type=MESH)
        return carry

    lax.fori_loop(1, ALL, greet, 0)
    for s in range(4):
        load(s).wait()
        load(4 + s).wait()

        def split(block, carry, s=s):
            for frame in (s, 4 + s):
                for part in range(2):
                    send[frame, part, block] = vv[pl.ds(frame * 1024 + block * 32 + part, 16, stride=2), :]
            return carry

        lax.fori_loop(0, ROWS, split, 0, unroll=2)
        if s == 0:
            pl.semaphore_wait(barrier, ALL - 1)

        def scatter(i, carry, s=s):
            r, c = any_peer(i, yr, yc)
            pltpu.make_async_remote_copy(
                src_ref=send.at[(c % 2) * 4 + s, c // 2, r], dst_ref=recv.at[s, me],
                send_sem=a2a_send, recv_sem=a2a_recv.at[s],
                device_id=(r, c), device_id_type=MESH,
            ).start()
            return carry

        lax.fori_loop(1, ALL, scatter, 0)
        recv[s, me] = send[(yc % 2) * 4 + s, yc // 2, yr]

    def gram(left, right, size):
        def add(i, carry):
            return carry + product_of_rows(left(i), right(i))

        return lax.fori_loop(0, size, add, jnp.zeros((128, 128), F32))

    def squares(block, size):
        def add(i, carry):
            x = block(i)
            return carry + jnp.sum(x * x, axis=0, keepdims=True)

        return lax.fori_loop(0, size, add, jnp.zeros((1, 128), F32))

    tiles = PIX // TILE
    a, b, c = roles(pairing_ref[0, yc])
    gram_p = None
    for s in range(4):
        if s == 3:
            gram_p = gram(lambda i: xt[a, tile(i), :], lambda i: xt[b, tile(i), :], tiles)
        whole = recv.at[s, pl.ds(0, ALL - 1)]
        pltpu.make_async_copy(whole, whole, a2a_recv.at[s]).wait()
        for g in range(16):
            flat[pl.ds(g * 128, 128), :] = recv[s, :, g, :].T

        def place(i, carry, s=s):
            for u in range(8):
                k = i * 8 + u
                xt[s, pl.ds(k, 1), :] = flat[pl.ds(order_ref[k] % PIX, 1), :]
            return carry

        lax.fori_loop(0, PIX // 8, place, 0)
        diag[pl.ds(s, 1), :] = squares(lambda i, s=s: xt[s, tile(i), :], tiles)

    gram_q = gram(lambda i: xt[c, tile(i), :], lambda i: xt[3, tile(i), :], tiles)

    def summed(t, first, second, diagonals):
        for r in range(16):
            parts[t, r, 0:8, :] = first[8 * r : 8 * r + 8]
            parts[t, 16 + r, 0:8, :] = second[8 * r : 8 * r + 8]
        for r in range(ROWS):
            for k in range(4):
                parts[t, r, 8 + k : 9 + k, :] = diagonals[k]

        def deal(i, carry):
            r = row_peer(i, yr)
            pltpu.make_async_remote_copy(
                src_ref=parts.at[t, r], dst_ref=arrived.at[t, yr],
                send_sem=rs_send.at[t], recv_sem=rs_recv.at[t],
                device_id=(r, yc), device_id_type=MESH,
            ).start()
            return carry

        lax.fori_loop(1, ROWS, deal, 0)
        arrived[t, yr] = parts[t, yr]
        whole = arrived.at[t, pl.ds(0, ROWS - 1)]
        pltpu.make_async_copy(whole, whole, rs_recv.at[t]).wait()
        total = arrived[t, 0]
        for r in range(1, ROWS):
            total = total + arrived[t, r]
        second_pair = yr >= 16
        left = jnp.where(second_pair, total[10:11], total[8:9])
        right = jnp.where(second_pair, total[11:12], total[9:10])
        spot = lax.broadcasted_iota(jnp.int32, (8, 128), 0) + 8 * (yr % 16)
        lane = lax.broadcasted_iota(jnp.int32, (8, 128), 1)
        left = jnp.sum(jnp.where(spot == lane, jnp.broadcast_to(left, (8, 128)), 0.0), axis=1, keepdims=True)
        mine = total[0:8] / (left + right)
        own[t] = mine
        coup[t, yr] = mine

        def share(i, carry):
            pltpu.make_async_remote_copy(
                src_ref=own.at[t], dst_ref=coup.at[t, yr],
                send_sem=ag_send.at[t], recv_sem=ag_recv.at[t],
                device_id=(row_peer(i, yr), yc), device_id_type=MESH,
            ).start()
            return carry

        lax.fori_loop(1, ROWS, share, 0)
        if t == 1:
            @pl.when(second_pair)
            def _():
                def lend(i, carry):
                    pltpu.make_async_remote_copy(
                        src_ref=own.at[t], dst_ref=coupn.at[yr - 16],
                        send_sem=ag_send.at[2], recv_sem=ag_recv.at[2],
                        device_id=(row_peer(i, yr), before), device_id_type=MESH,
                    ).start()
                    return carry

                lax.fori_loop(0, ROWS, lend, 0)

        whole = coup.at[t, pl.ds(0, ROWS - 1)]
        pltpu.make_async_copy(whole, whole, ag_recv.at[t]).wait()
        both = coup[t].reshape(256, 128)
        return both[:128], both[128:]

    first, second = summed(
        0, gram_p, gram_q,
        (diag[pl.ds(a, 1), :], diag[pl.ds(b, 1), :], diag[pl.ds(c, 1), :], diag[3:4, :]),
    )
    for k, (top, cross, down, low) in enumerate(rotations((first, second), state)):
        rot[k, :128, :128] = top
        rot[k, :128, 128:] = cross
        rot[k, 128:, :128] = down
        rot[k, 128:, 128:] = low

    def forward(i):
        return pltpu.make_async_remote_copy(
            src_ref=yy.at[3, tile(i)], dst_ref=z.at[tile(i)],
            send_sem=z_send.at[i], recv_sem=z_recv.at[i],
            device_id=(yr, after), device_id_type=MESH,
        )

    def turn_second(i, carry):
        x = jnp.concatenate([xt[c, tile(i), :], xt[3, tile(i), :]], axis=1)
        turned = product(x, rot[1])
        yy[3, tile(i), :] = turned[:, 128:]
        yy[2, tile(i), :] = turned[:, :128]
        forward(i).start()
        return carry

    lax.fori_loop(0, tiles, turn_second, 0)

    def turn_first(i, carry):
        x = jnp.concatenate([xt[a, tile(i), :], xt[b, tile(i), :]], axis=1)
        turned = product(x, rot[0])
        yy[0, tile(i), :] = turned[:, :128]
        yy[1, tile(i), :] = turned[:, 128:]
        return carry

    lax.fori_loop(0, tiles, turn_first, 0)
    keep = pltpu.make_async_copy(yy, y_ref, out_sem.at[0])
    keep.start()

    def role_of(slot):
        return jnp.where(slot == a, 0, jnp.where(slot == b, 1, 2))

    a2, b2, c2 = (role_of(slot) for slot in roles(pairing_ref[1, yc]))
    gram_p = gram(lambda i: yy[a2, tile(i), :], lambda i: yy[b2, tile(i), :], tiles)
    lows = [squares(lambda i, k=k: yy[k, tile(i), :], tiles) for k in (a2, b2, c2)]

    def stage(i, carry):
        q[tile(i), :] = yy[c2, tile(i), :]
        return carry

    lax.fori_loop(0, tiles, stage, 0)

    def meet(i, carry):
        total, square = carry
        forward(i).wait_recv()
        block = z[tile(i), :]
        return (
            total + product_of_rows(q[tile(i), :], block),
            square + jnp.sum(block * block, axis=0, keepdims=True),
        )

    gram_q, last = lax.fori_loop(
        0, tiles, meet, (jnp.zeros((128, 128), F32), jnp.zeros((1, 128), F32))
    )
    back = pltpu.make_async_remote_copy(
        src_ref=q, dst_ref=qn_ref, send_sem=q_send, recv_sem=q_recv,
        device_id=(yr, before), device_id_type=MESH,
    )
    back.start()
    keep_z = pltpu.make_async_copy(z, z_ref, out_sem.at[1])
    keep_z.start()
    first, second = summed(1, gram_p, gram_q, (*lows, last))
    pltpu.make_async_copy(coupn, coupn, ag_recv.at[2]).wait()
    third = coupn[...].reshape(128, 128)
    turns = rotations((first, second, third), state)
    turn_ref[:128, 0:128] = turns[0][0]
    turn_ref[:128, 128:256] = turns[0][1]
    turn_ref[128:, 0:128] = turns[0][2]
    turn_ref[128:, 128:256] = turns[0][3]
    turn_ref[:128, 256:384] = turns[1][0]
    turn_ref[128:, 256:384] = turns[1][2]
    turn_ref[:128, 384:512] = turns[2][1]
    turn_ref[128:, 384:512] = turns[2][3]

    keep.wait()
    keep_z.wait()
    back.wait()

    def drain(i, carry):
        forward(i).wait_send()
        return carry

    lax.fori_loop(0, tiles, drain, 0)
    for s in range(4):
        whole = recv.at[s, pl.ds(0, ALL - 1)]
        pltpu.make_async_copy(whole, whole, a2a_send).wait()
    for t in range(2):
        whole = arrived.at[t, pl.ds(0, ROWS - 1)]
        pltpu.make_async_copy(whole, whole, rs_send.at[t]).wait()
        whole = coup.at[t, pl.ds(0, ROWS - 1)]
        pltpu.make_async_copy(whole, whole, ag_send.at[t]).wait()

    @pl.when(yr >= 16)
    def _():
        whole = coup.at[1]
        pltpu.make_async_copy(whole, whole, ag_send.at[2]).wait()


def two_steps(v, order, pairing):
    tiles = PIX // TILE
    dma = pltpu.SemaphoreType.DMA
    return pl.pallas_call(
        steps_kernel,
        out_shape=(
            jax.ShapeDtypeStruct((4, PIX, 128), F32),
            jax.ShapeDtypeStruct((PIX, 128), F32),
            jax.ShapeDtypeStruct((PIX, 128), F32),
            jax.ShapeDtypeStruct((256, 512), F32),
        ),
        in_specs=[ANY, SMEM, SMEM],
        out_specs=(ANY, ANY, ANY, pl.BlockSpec(memory_space=pltpu.VMEM)),
        scratch_shapes=[
            pltpu.VMEM((8192, 128), F32),
            pltpu.VMEM((8, 2, ROWS, 16, 128), F32),
            pltpu.VMEM((4, ALL, 16, 128), F32),
            pltpu.VMEM((PIX, 128), F32),
            pltpu.VMEM((4, PIX, 128), F32),
            pltpu.VMEM((4, PIX, 128), F32),
            pltpu.VMEM((PIX, 128), F32),
            pltpu.VMEM((PIX, 128), F32),
            pltpu.VMEM((4, 128), F32),
            pltpu.VMEM((2, ROWS, 12, 128), F32),
            pltpu.VMEM((2, ROWS, 12, 128), F32),
            pltpu.VMEM((2, 8, 128), F32),
            pltpu.VMEM((2, ROWS, 8, 128), F32),
            pltpu.VMEM((16, 8, 128), F32),
            pltpu.VMEM((2, 256, 256), F32),
            pltpu.VMEM((6, 256, 128), F32),
            dma((8,)), dma((2,)), dma, dma((4,)), dma((2,)), dma((2,)), dma((3,)), dma((3,)),
            dma((tiles,)), dma((tiles,)), dma, dma,
        ],
        compiler_params=pltpu.CompilerParams(
            collective_id=0, has_side_effects=True, vmem_limit_bytes=48 * 2**20
        ),
    )(v, order, pairing)


def finish_kernel(y_ref, z_ref, qn_ref, turn_ref, pairing_ref, out_ref):
    yc = lax.axis_index("cols")
    a, b, c = roles(pairing_ref[0, yc])
    slots = roles(pairing_ref[1, yc])
    a2, b2, c2 = (jnp.where(slot == a, 0, jnp.where(slot == b, 1, 2)) for slot in slots)
    at = [pl.ds(pl.multiple_of(slot * 128, 128), 128) for slot in slots]
    turned = product(jnp.concatenate([y_ref[a2], y_ref[b2]], axis=1), turn_ref[:, 0:256])
    out_ref[:, at[0]] = turned[:, :128]
    out_ref[:, at[1]] = turned[:, 128:]
    out_ref[:, at[2]] = product(jnp.concatenate([y_ref[c2], z_ref[...]], axis=1), turn_ref[:, 256:384])
    out_ref[:, 384:512] = product(jnp.concatenate([qn_ref[...], y_ref[3]], axis=1), turn_ref[:, 384:512])


def finish(y, z, qn, turn, pairing):
    rows = 512
    return pl.pallas_call(
        finish_kernel,
        grid=(PIX // rows,),
        out_shape=jax.ShapeDtypeStruct((PIX, 512), F32),
        in_specs=[
            pl.BlockSpec((4, rows, 128), lambda i: (0, i, 0)),
            pl.BlockSpec((rows, 128), lambda i: (i, 0)),
            pl.BlockSpec((rows, 128), lambda i: (i, 0)),
            pl.BlockSpec((256, 512), lambda i: (0, 0)),
            SMEM,
        ],
        out_specs=pl.BlockSpec((rows, 512), lambda i: (i, 0)),
        compiler_params=pltpu.CompilerParams(vmem_limit_bytes=24 * 2**20),
    )(y, z, qn, turn, pairing)


def body(tracks, pixel_order, pairing):
    v = tracks.reshape(8, 2, 512, 128).transpose(0, 2, 1, 3).reshape(8192, 128)
    return finish(*two_steps(v, pixel_order, pairing), pairing)


def solution(mesh):
    placed = (P(("rows", "cols"), None, None), P("rows"), P())
    return jax.shard_map(
        body, mesh=mesh, in_specs=placed, out_specs=P("rows", "cols"), check_vma=False
    )
```

profile of v0, /device:TPU:1, one launch (start us, length us, event | category | flops | bytes accessed | tf_op | source)
XLA Modules:
  0.0 152.6 jit_solution(2212117004144684356)
XLA Ops:
  0.0 0.0 copy-start.1
  0.0 0.7 copy-done.1
  0.7 0.0 copy-start.2
  0.7 0.7 copy-done.2
  1.4 143.8 %shard_map.37 = (f32[4,2048,128]{2,1,0:T(8,128)}, f32[2048,128]{1,0:T(8,128)S(1)}, f32[2048,128]{1,0:T(8,128)S(1)}, f32[256,512]{1,0:T(8,128)S(1)}) custom-call(f32[8192,128]{1,0:T(8,128)} %bitcast.5, s32[2048]{0:T(1024)S(1)} %copy-done.1, s32[2,4]{1,0:T(2,128)S(1)} %copy-done.2), custom_call_target="tpu_custom_call" | custom-call | tf_op jit(solution)/shard_map/pallas_call | solution.py:346
  145.2 0.0 copy-start
  145.2 2.2 %copy-done = f32[4,2048,128]{2,1,0:T(8,128)S(1)} copy-done((f32[4,2048,128]{2,1,0:T(8,128)S(1)}, f32[4,2048,128]{2,1,0:T(8,128)}, u32[]{:S(2)}) %copy-start) | copy-done | bytes 4194328
  147.4 5.2 %shard_map.38 = f32[2048,512]{1,0:T(8,128)} custom-call(f32[4,2048,128]{2,1,0:T(8,128)S(1)} %copy-done, f32[2048,128]{1,0:T(8,128)S(1)} %get-tuple-element.10.z_ref, f32[2048,128]{1,0:T(8,128)S(1)} %get-tuple-element.11.qn_ref, f32[256,512]{1,0:T(8,128)S(1)} %get-tuple-element.12.turn_ref, s32[2,4]{1,0:T(2,128)S(1)} %copy-done.2), custom_call_target="tpu_custom_call" | custom-call | tf_op jit(solution)/shard_map/pallas_call | solution.py:397
Async XLA Ops:
  0.0 0.7 copy-start.1
  0.7 0.7 copy-start.2
  145.2 2.2 %copy-start = (f32[4,2048,128]{2,1,0:T(8,128)S(1)}, f32[4,2048,128]{2,1,0:T(8,128)}, u32[]{:S(2)}) copy-start(f32[4,2048,128]{2,1,0:T(8,128)} %get-tuple-element.9.y_ref) | copy-start | bytes 12582916
where the time goes:
time: 153 us
  Pallas kernels  149 us (97%)
  local copies, waits for them, and re-layouts  3.56 us (2%)
    pallas_call x1, Pallas kernels, two_steps(): pl.pallas_call(steps_kernel, out_shape=(jax.ShapeDtypeStruct((4, PIX, 128...  144 us
    pallas_call x1, Pallas kernels, finish(): pl.pallas_call(finish_kernel, grid=(PIX // rows,), out_shape=jax.ShapeDty...  5.17 us
    unnamed x6, local copies, waits for them, and re-layouts  3.56 us

commit v1 on v0

v1 whole, which is shorter than its diff:
```python
import jax
import jax.numpy as jnp
from jax import lax
from jax.experimental import pallas as pl
from jax.experimental.pallas import tpu as pltpu
from jax.sharding import PartitionSpec as P

F32 = jnp.float32
MESH = pl.DeviceIdType.MESH
ANY = pl.BlockSpec(memory_space=pl.ANY)
SMEM = pl.BlockSpec(memory_space=pltpu.SMEM)
INNER = pl.BlockSpec(memory_space=pltpu.VMEM)
HIGH = lax.Precision.HIGH
NS_STEPS = 6
ROWS = 32
COLS = 4
ALL = ROWS * COLS
PIX = 2048
TILE = 512
TILES = PIX // TILE
VMEM = 46 * 2**20


def product(a, b):
    return jnp.dot(a, b, precision=HIGH, preferred_element_type=F32)


def product_of_rows(a, b):
    return lax.dot_general(a, b, (((0,), (0,)), ((), ())), precision=HIGH, preferred_element_type=F32)


def any_peer(i, yr, yc):
    first, second, third = (i >> 1) & 3, (i >> 3) & 3, i >> 5
    y = ((yr >> 3) + first + second) & 3
    x = (((yr >> 1) & 2) + (yc >> 1) + first) & 3
    z = (yr + first + third + 2 * second) & 3
    return (y << 3) + ((x >> 1) << 2) + z, ((x & 1) << 1) + ((yc + i) & 1)


def row_peer(i, yr):
    y = ((yr >> 3) + (i >> 2)) & 3
    x = ((yr >> 2) + (i >> 4)) & 1
    z = (yr + i) & 3
    return (y << 3) + (x << 2) + z


def roles(choice):
    low = jnp.where(choice == 2, 1, 0)
    high = jnp.where(choice == 0, 1, 2)
    return low, high, 2 - choice


def tile(i):
    if isinstance(i, int):
        return pl.ds(i * TILE, TILE)
    return pl.ds(pl.multiple_of(i * TILE, TILE), TILE)


def exact(a, b):
    return jnp.dot(a, b, precision=lax.Precision.HIGHEST, preferred_element_type=F32)


def rotations(couplings, state, weight):
    size = 128
    row = lax.broadcasted_iota(jnp.int32, (size, size), 0)
    col = lax.broadcasted_iota(jnp.int32, (size, size), 1)
    eye = jnp.where(row == col, 1.0, 0.0).astype(F32)
    count = 2 * len(couplings)
    flipped = [c.T for c in couplings]
    for k, c in enumerate(couplings):
        total = 1.0 + jnp.sum(jnp.sum(c * c, axis=1, keepdims=True), axis=0, keepdims=True)
        start = eye * (1.0 / jnp.sqrt(total))
        for m, square in ((2 * k, exact(c, flipped[k])), (2 * k + 1, exact(flipped[k], c))):
            weight[m] = eye + square
            state[m, :size, :] = (eye + square) / total
            state[m, size:, :] = start

    def step(_, carry):
        held = [state[m] for m in range(count)]
        factors = [1.5 * eye - 0.5 * h[:size] for h in held]
        once = [product(h, f) for h, f in zip(held, factors)]
        twice = [product(o[:size], f) for o, f in zip(once, factors)]
        for m in range(count):
            state[m, :size, :] = twice[m]
            state[m, size:, :] = once[m][size:]
        return carry

    lax.fori_loop(0, NS_STEPS - 1, step, 0)
    half = [state[m, size:, :] for m in range(count)]
    met = [exact(weight[m], half[m]) for m in range(count)]
    inner = [exact(half[m], met[m]) for m in range(count)]
    last = [exact(half[m], 1.5 * eye - 0.5 * inner[m]) for m in range(count)]
    out = []
    for k, c in enumerate(couplings):
        cross = exact(last[2 * k], c)
        out.append((last[2 * k], cross, -cross.T, last[2 * k + 1]))
    return out


def steps_kernel(
    v_ref, order_ref, pairing_ref, y_ref, z_ref, qn_ref, turn_ref,
    vv, send, recv, flat, xt, yy, zc, z3, z, q, diag, parts, arrived, own, coup, coupn, rot, state, weight,
    load_sem, out_sem, a2a_send, a2a_recv, rs_send, rs_recv, ag_send, ag_recv, lend_send, lend_recv,
    z_send, z_recv, q_send, q_recv,
):
    yr, yc = lax.axis_index("rows"), lax.axis_index("cols")
    me = yr * COLS + yc
    after, before = (yc + 1) & 3, (yc + 3) & 3
    barrier = pltpu.get_barrier_semaphore()

    def load(frame):
        lines = pl.ds(frame * 1024, 1024)
        return pltpu.make_async_copy(v_ref.at[lines], vv.at[lines], load_sem.at[frame])

    for s in range(4):
        load(s).start()
        load(4 + s).start()

    def greet(i, carry):
        pl.semaphore_signal(barrier, inc=1, device_id=any_peer(i, yr, yc), device_id_type=MESH)
        return carry

    lax.fori_loop(1, ALL, greet, 0, unroll=9)
    for s in range(4):
        load(s).wait()
        load(4 + s).wait()

        def split(block, carry, s=s):
            for frame in (s, 4 + s):
                for part in range(2):
                    send[frame, part, block] = vv[pl.ds(frame * 1024 + block * 32 + part, 16, stride=2), :]
            return carry

        lax.fori_loop(0, ROWS, split, 0, unroll=2)
        if s == 0:
            pl.semaphore_wait(barrier, ALL - 1)

        def scatter(i, carry, s=s):
            r, c = any_peer(i, yr, yc)
            pltpu.make_async_remote_copy(
                src_ref=send.at[((c & 1) << 2) + s, c >> 1, r], dst_ref=recv.at[s, me],
                send_sem=a2a_send, recv_sem=a2a_recv.at[s],
                device_id=(r, c), device_id_type=MESH,
            ).start()
            return carry

        lax.fori_loop(1, ALL, scatter, 0)
        recv[s, me] = send[((yc & 1) << 2) + s, yc >> 1, yr]

    def gram(left, right):
        def add(i, carry):
            return carry + product_of_rows(left(i), right(i))

        return lax.fori_loop(0, TILES, add, jnp.zeros((128, 128), F32))

    def squares(block):
        def add(i, carry):
            x = block(i)
            return carry + jnp.sum(x * x, axis=0, keepdims=True)

        return lax.fori_loop(0, TILES, add, jnp.zeros((1, 128), F32))

    def place(s):
        def move(i, carry):
            for u in range(16):
                k = i * 16 + u
                xt[s, pl.ds(k, 1), :] = flat[s, pl.ds(order_ref[k] & (PIX - 1), 1), :]
            return carry

        lax.fori_loop(0, PIX // 16, move, 0)

    a, b, c = roles(pairing_ref[0, yc])
    gram_p = None
    for s in range(4):
        if s == 3:
            gram_p = gram(lambda i: flat[a, tile(i), :], lambda i: flat[b, tile(i), :])
        whole = recv.at[s, pl.ds(0, ALL - 1)]
        pltpu.make_async_copy(whole, whole, a2a_recv.at[s]).wait()
        for g in range(16):
            flat[s, pl.ds(g * 128, 128), :] = recv[s, :, g, :].T
        diag[pl.ds(s, 1), :] = squares(lambda i, s=s: flat[s, tile(i), :])
        if s < 3:
            place(s)

    def summed(t, first, second, diagonals, early, late):
        low = jnp.concatenate(diagonals, axis=0)
        for r in range(16):
            parts[t, r, 0:8, :] = first[8 * r : 8 * r + 8]
            parts[t, 16 + r, 0:8, :] = second[8 * r : 8 * r + 8]
        for r in range(ROWS):
            parts[t, r, 8:12, :] = low

        def deal(i, carry):
            r = row_peer(i, yr)
            pltpu.make_async_remote_copy(
                src_ref=parts.at[t, r], dst_ref=arrived.at[t, yr],
                send_sem=rs_send.at[t], recv_sem=rs_recv.at[t],
                device_id=(r, yc), device_id_type=MESH,
            ).start()
            return carry

        lax.fori_loop(1, ROWS, deal, 0, unroll=True)
        arrived[t, yr] = parts[t, yr]
        early()
        whole = arrived.at[t, pl.ds(0, ROWS - 1)]
        pltpu.make_async_copy(whole, whole, rs_recv.at[t]).wait()
        total = arrived[t, 0]
        for r in range(1, ROWS):
            total = total + arrived[t, r]
        second_pair = yr >= 16
        left = jnp.where(second_pair, total[10:11], total[8:9])
        right = jnp.where(second_pair, total[11:12], total[9:10])
        spot = lax.broadcasted_iota(jnp.int32, (8, 128), 0) + 8 * (yr & 15)
        lane = lax.broadcasted_iota(jnp.int32, (8, 128), 1)
        left = jnp.sum(jnp.where(spot == lane, jnp.broadcast_to(left, (8, 128)), 0.0), axis=1, keepdims=True)
        mine = total[0:8] / (left + right)
        own[t] = mine
        coup[t, yr] = mine

        def share(i, carry):
            pltpu.make_async_remote_copy(
                src_ref=own.at[t], dst_ref=coup.at[t, yr],
                send_sem=ag_send.at[t], recv_sem=ag_recv.at[t],
                device_id=(row_peer(i, yr), yc), device_id_type=MESH,
            ).start()
            return carry

        lax.fori_loop(1, ROWS, share, 0, unroll=True)

        @pl.when(second_pair)
        def _():
            def lend(i, carry):
                pltpu.make_async_remote_copy(
                    src_ref=own.at[t], dst_ref=coupn.at[t, yr - 16],
                    send_sem=lend_send.at[t], recv_sem=lend_recv.at[t],
                    device_id=(row_peer(i, yr), before if t else after), device_id_type=MESH,
                ).start()
                return carry

            lax.fori_loop(0, ROWS, lend, 0, unroll=True)

        late()
        whole = coup.at[t, pl.ds(0, ROWS - 1)]
        pltpu.make_async_copy(whole, whole, ag_recv.at[t]).wait()
        whole = coupn.at[t]
        pltpu.make_async_copy(whole, whole, lend_recv.at[t]).wait()
        both = coup[t].reshape(256, 128)
        return both[:128], both[128:], coupn[t].reshape(128, 128)

    half = PIX // 2
    upper, lower = pl.ds(0, half), pl.ds(half, half)
    raw = TILES - 1

    def forward(k):
        at = pl.ds(k % raw * TILE, TILE)
        pairs = ((q.at[at], zc.at[at]), (xt.at[3, at], z3.at[at]))
        src, dst = pairs[k // raw] if k < 2 * raw else (yy.at[3, pl.ds(raw * TILE, TILE)], z.at[pl.ds(raw * TILE, TILE)])
        return pltpu.make_async_remote_copy(
            src_ref=src, dst_ref=dst, send_sem=z_send.at[k], recv_sem=z_recv.at[k],
            device_id=(yr, after), device_id_type=MESH,
        )

    q[pl.ds(0, TILE), :] = xt[c, pl.ds(0, TILE), :]
    forward(0).start()
    gram_q = gram(lambda i: flat[c, tile(i), :], lambda i: flat[3, tile(i), :])

    def early_first():
        for k in range(1, raw):
            q[pl.ds(k * TILE, TILE), :] = xt[c, pl.ds(k * TILE, TILE), :]
            forward(k).start()
        place(3)

    def late_first():
        for k in range(raw, 2 * raw):
            forward(k).start()

    first, second, third = summed(
        0, gram_p, gram_q,
        (diag[pl.ds(a, 1), :], diag[pl.ds(b, 1), :], diag[pl.ds(c, 1), :], diag[3:4, :]),
        early_first, late_first,
    )
    for k, (top, cross, down, low) in enumerate(rotations((first, second, third), state, weight)):
        rot[k, :128, :128] = top
        rot[k, :128, 128:] = cross
        rot[k, 128:, :128] = down
        rot[k, 128:, 128:] = low

    def turn_second(i):
        x = jnp.concatenate([xt[c, tile(i), :], xt[3, tile(i), :]], axis=1)
        turned = product(x, rot[1])
        yy[3, tile(i), :] = turned[:, 128:]
        yy[2, tile(i), :] = turned[:, :128]

    def turn_first(i):
        x = jnp.concatenate([xt[a, tile(i), :], xt[b, tile(i), :]], axis=1)
        turned = product(x, rot[0])
        yy[0, tile(i), :] = turned[:, :128]
        yy[1, tile(i), :] = turned[:, 128:]

    def turn_own(i, carry):
        turn_first(i)
        turn_second(i)
        return carry

    turn_second(raw)
    forward(2 * raw).start()
    turn_first(raw)
    lax.fori_loop(0, raw, turn_own, 0)
    keep = pltpu.make_async_copy(yy, y_ref, out_sem.at[0])
    keep.start()

    def role_of(slot):
        return jnp.where(slot == a, 0, jnp.where(slot == b, 1, 2))

    a2, b2, c2 = (role_of(slot) for slot in roles(pairing_ref[1, yc]))
    gram_p = gram(lambda i: yy[a2, tile(i), :], lambda i: yy[b2, tile(i), :])
    lows = [squares(lambda i, k=k: yy[k, tile(i), :]) for k in (a2, b2, c2)]

    for k in range(2 * raw):
        forward(k).wait_recv()

    def meet(i, block, carry):
        total, square = carry
        return (
            total + product_of_rows(yy[c2, tile(i), :], block),
            square + jnp.sum(block * block, axis=0, keepdims=True),
        )

    def turn_and_meet(i, carry):
        x = jnp.concatenate([zc[tile(i), :], z3[tile(i), :]], axis=1)
        block = product(x, rot[2, :, 128:])
        z[tile(i), :] = block
        return meet(i, block, carry)

    met = lax.fori_loop(
        0, raw, turn_and_meet, (jnp.zeros((128, 128), F32), jnp.zeros((1, 128), F32))
    )
    forward(2 * raw).wait_recv()
    gram_q, last = meet(raw, z[tile(raw), :], met)
    keep_z = pltpu.make_async_copy(z, z_ref, out_sem.at[1])
    keep_z.start()
    for k in range(raw):
        forward(k).wait_send()

    def backward(k):
        part = (upper, lower)[k]
        return pltpu.make_async_remote_copy(
            src_ref=q.at[part], dst_ref=qn_ref.at[part], send_sem=q_send.at[k], recv_sem=q_recv.at[k],
            device_id=(yr, before), device_id_type=MESH,
        )

    def early_second():
        q[upper, :] = yy[c2, upper, :]
        backward(0).start()
        q[lower, :] = yy[c2, lower, :]

    first, second, third = summed(
        1, gram_p, gram_q, (*lows, last), early_second, lambda: backward(1).start()
    )
    turns = rotations((first, second, third), state, weight)
    turn_ref[:128, 0:128] = turns[0][0]
    turn_ref[:128, 128:256] = turns[0][1]
    turn_ref[128:, 0:128] = turns[0][2]
    turn_ref[128:, 128:256] = turns[0][3]
    turn_ref[:128, 256:384] = turns[1][0]
    turn_ref[128:, 256:384] = turns[1][2]
    turn_ref[:128, 384:512] = turns[2][1]
    turn_ref[128:, 384:512] = turns[2][3]

    keep.wait()
    keep_z.wait()
    for k in range(raw, 2 * raw + 1):
        forward(k).wait_send()
    for k in range(2):
        backward(k).wait()
    for s in range(4):
        whole = recv.at[s, pl.ds(0, ALL - 1)]
        pltpu.make_async_copy(whole, whole, a2a_send).wait()
    for t in range(2):
        whole = arrived.at[t, pl.ds(0, ROWS - 1)]
        pltpu.make_async_copy(whole, whole, rs_send.at[t]).wait()
        whole = coup.at[t, pl.ds(0, ROWS - 1)]
        pltpu.make_async_copy(whole, whole, ag_send.at[t]).wait()

    @pl.when(yr >= 16)
    def _():
        for t in range(2):
            whole = coup.at[t]
            pltpu.make_async_copy(whole, whole, lend_send.at[t]).wait()


def two_steps(v, order, pairing):
    dma = pltpu.SemaphoreType.DMA
    return pl.pallas_call(
        steps_kernel,
        out_shape=(
            jax.ShapeDtypeStruct((4, PIX, 128), F32),
            jax.ShapeDtypeStruct((PIX, 128), F32),
            jax.ShapeDtypeStruct((PIX, 128), F32),
            jax.ShapeDtypeStruct((256, 512), F32),
        ),
        in_specs=[ANY, SMEM, SMEM],
        out_specs=(ANY, ANY, ANY, pl.BlockSpec(memory_space=pltpu.VMEM)),
        scratch_shapes=[
            pltpu.VMEM((8192, 128), F32),
            pltpu.VMEM((8, 2, ROWS, 16, 128), F32),
            pltpu.VMEM((4, ALL, 16, 128), F32),
            pltpu.VMEM((4, PIX, 128), F32),
            pltpu.VMEM((4, PIX, 128), F32),
            pltpu.VMEM((4, PIX, 128), F32),
            pltpu.VMEM((PIX, 128), F32),
            pltpu.VMEM((PIX, 128), F32),
            pltpu.VMEM((PIX, 128), F32),
            pltpu.VMEM((PIX, 128), F32),
            pltpu.VMEM((4, 128), F32),
            pltpu.VMEM((2, ROWS, 12, 128), F32),
            pltpu.VMEM((2, ROWS, 12, 128), F32),
            pltpu.VMEM((2, 8, 128), F32),
            pltpu.VMEM((2, ROWS, 8, 128), F32),
            pltpu.VMEM((2, 16, 8, 128), F32),
            pltpu.VMEM((3, 256, 256), F32),
            pltpu.VMEM((6, 256, 128), F32),
            pltpu.VMEM((6, 128, 128), F32),
            dma((8,)), dma((2,)), dma, dma((4,)), dma((2,)), dma((2,)), dma((2,)), dma((2,)), dma((2,)), dma((2,)),
            dma((2 * TILES - 1,)), dma((2 * TILES - 1,)), dma((2,)), dma((2,)),
        ],
        compiler_params=pltpu.CompilerParams(
            collective_id=0, has_side_effects=True, vmem_limit_bytes=VMEM
        ),
    )(v, order, pairing)


def finish_kernel(y_ref, z_ref, qn_ref, turn_ref, pairing_ref, out_ref):
    yc = lax.axis_index("cols")
    a, b, c = roles(pairing_ref[0, yc])
    slots = roles(pairing_ref[1, yc])
    a2, b2, c2 = (jnp.where(slot == a, 0, jnp.where(slot == b, 1, 2)) for slot in slots)
    at = [pl.ds(pl.multiple_of(slot * 128, 128), 128) for slot in slots]
    here = tile(pl.program_id(0))

    def turned(first, second, columns):
        return product(jnp.concatenate([first[here, :], second[here, :]], axis=1), turn_ref[:, columns])

    pair = turned(y_ref.at[a2], y_ref.at[b2], pl.ds(0, 256))
    out_ref[:, at[0]] = pair[:, :128]
    out_ref[:, at[1]] = pair[:, 128:]
    out_ref[:, at[2]] = turned(y_ref.at[c2], z_ref, pl.ds(256, 128))
    out_ref[:, 384:512] = turned(qn_ref, y_ref.at[3], pl.ds(384, 128))


def finish(y, z, qn, turn, pairing):
    rows = TILE
    return pl.pallas_call(
        finish_kernel,
        grid=(PIX // rows,),
        out_shape=jax.ShapeDtypeStruct((PIX, 512), F32),
        in_specs=[INNER, INNER, INNER, INNER, SMEM],
        out_specs=pl.BlockSpec((rows, 512), lambda i: (i, 0)),
        compiler_params=pltpu.CompilerParams(vmem_limit_bytes=24 * 2**20),
    )(y, z, qn, turn, pairing)


def body(tracks, pixel_order, pairing):
    v = tracks.reshape(8, 2, 512, 128).transpose(0, 2, 1, 3).reshape(8192, 128)
    return finish(*two_steps(v, pixel_order, pairing), pairing)


def solution(mesh):
    placed = (P(("rows", "cols"), None, None), P("rows"), P())
    return jax.shard_map(
        body, mesh=mesh, in_specs=placed, out_specs=P("rows", "cols"), check_vma=False
    )
```

time: 153 us -> 119 us (0.78)
  Pallas kernels: 149 us -> 117 us
  local copies, waits for them, and re-layouts: 3.56 us -> 1.37 us
    pallas_call x1, Pallas kernels: 144 us -> 112 us  [two_steps(): pl.pallas_call(steps_kernel, out_shape=(jax.ShapeDtypeStruct((4, PIX, 128...]
    unnamed x6 -> x4, local copies, waits for them, and re-layouts: 3.56 us -> 1.37 us
where the time goes in v1:
time: 119 us
  Pallas kernels  117 us (98%)
  local copies, waits for them, and re-layouts  1.37 us (1%)
    pallas_call x1, Pallas kernels, two_steps(): pl.pallas_call(steps_kernel, out_shape=(jax.ShapeDtypeStruct((4, PIX, 128...  112 us
    pallas_call x1, Pallas kernels, finish(): pl.pallas_call(finish_kernel, grid=(PIX // rows,), out_shape=jax.ShapeDty...  5.05 us

profile of v1, /device:TPU:1, one launch (start us, length us, event | category | flops | bytes accessed | tf_op | source)
XLA Modules:
  0.0 118.8 jit_solution(12213278023099723048)
XLA Ops:
  0.0 0.0 copy-start
  0.0 0.7 copy-done
  0.7 0.0 copy-start.1
  0.7 0.7 copy-done.1
  1.4 112.4 %shard_map.37 = (f32[4,2048,128]{2,1,0:T(8,128)S(1)}, f32[2048,128]{1,0:T(8,128)S(1)}, f32[2048,128]{1,0:T(8,128)S(1)}, f32[256,512]{1,0:T(8,128)S(1)}) custom-call(f32[8192,128]{1,0:T(8,128)} %bitcast.5, s32[2048]{0:T(1024)S(1)} %copy-done, s32[2,4]{1,0:T(2,128)S(1)} %copy-done.1), custom_call_target="tpu_custom_call" | custom-call | tf_op jit(solution)/shard_map/pallas_call | solution.py:394
  113.8 5.0 %shard_map.38 = f32[2048,512]{1,0:T(8,128)} custom-call(f32[4,2048,128]{2,1,0:T(8,128)S(1)} %get-tuple-element.9.y_ref, f32[2048,128]{1,0:T(8,128)S(1)} %get-tuple-element.10.z_ref, f32[2048,128]{1,0:T(8,128)S(1)} %get-tuple-element.11.qn_ref, f32[256,512]{1,0:T(8,128)S(1)} %get-tuple-element.12.turn_ref, s32[2,4]{1,0:T(2,128)S(1)} %copy-done.1), custom_call_target="tpu_custom_call" | custom-call | tf_op jit(solution)/shard_map/pallas_call | solution.py:453
Async XLA Ops:
  0.0 0.7 copy-start
  0.7 0.7 copy-start.1

commit v2 on v1

--- a/solution.py
+++ b/solution.py
@@ -44,6 +44,14 @@
     return (y << 3) + (x << 2) + z
 
 
+def hops(i):
+    ring = (0, 1, 2, 1)
+    return ring[i & 3] + ring[i >> 2 & 3] + 2 * (i >> 4)
+
+
+FAR_FIRST = sorted(range(ROWS), key=hops, reverse=True)
+
+
 def roles(choice):
     low = jnp.where(choice == 2, 1, 0)
     high = jnp.where(choice == 0, 1, 2)
@@ -85,14 +93,16 @@
             state[m, size:, :] = once[m][size:]
         return carry
 
-    lax.fori_loop(0, NS_STEPS - 1, step, 0)
+    lax.fori_loop(0, NS_STEPS - 1, step, 0, unroll=True)
     half = [state[m, size:, :] for m in range(count)]
     met = [exact(weight[m], half[m]) for m in range(count)]
     inner = [exact(half[m], met[m]) for m in range(count)]
-    last = [exact(half[m], 1.5 * eye - 0.5 * inner[m]) for m in range(count)]
+    crossed = [exact(half[2 * k], c) for k, c in enumerate(couplings)]
+    factors = [1.5 * eye - 0.5 * n for n in inner]
+    last = [exact(h, f) for h, f in zip(half, factors)]
     out = []
-    for k, c in enumerate(couplings):
-        cross = exact(last[2 * k], c)
+    for k in range(len(couplings)):
+        cross = exact(factors[2 * k], crossed[k])
         out.append((last[2 * k], cross, -cross.T, last[2 * k + 1]))
     return out
 
@@ -183,23 +193,20 @@
             place(s)
 
     def summed(t, first, second, diagonals, early, late):
-        low = jnp.concatenate(diagonals, axis=0)
+        lows = [jnp.concatenate(diagonals[k : k + 2], axis=0) for k in (0, 2)]
         for r in range(16):
             parts[t, r, 0:8, :] = first[8 * r : 8 * r + 8]
             parts[t, 16 + r, 0:8, :] = second[8 * r : 8 * r + 8]
         for r in range(ROWS):
-            parts[t, r, 8:12, :] = low
-
-        def deal(i, carry):
+            parts[t, r, 8:10, :] = lows[r // 16]
+
+        for i in FAR_FIRST[:-1]:
             r = row_peer(i, yr)
             pltpu.make_async_remote_copy(
                 src_ref=parts.at[t, r], dst_ref=arrived.at[t, yr],
                 send_sem=rs_send.at[t], recv_sem=rs_recv.at[t],
                 device_id=(r, yc), device_id_type=MESH,
             ).start()
-            return carry
-
-        lax.fori_loop(1, ROWS, deal, 0, unroll=True)
         arrived[t, yr] = parts[t, yr]
         early()
         whole = arrived.at[t, pl.ds(0, ROWS - 1)]
@@ -208,8 +215,7 @@
         for r in range(1, ROWS):
             total = total + arrived[t, r]
         second_pair = yr >= 16
-        left = jnp.where(second_pair, total[10:11], total[8:9])
-        right = jnp.where(second_pair, total[11:12], total[9:10])
+        left, right = total[8:9], total[9:10]
         spot = lax.broadcasted_iota(jnp.int32, (8, 128), 0) + 8 * (yr & 15)
         lane = lax.broadcasted_iota(jnp.int32, (8, 128), 1)
         left = jnp.sum(jnp.where(spot == lane, jnp.broadcast_to(left, (8, 128)), 0.0), axis=1, keepdims=True)
@@ -217,27 +223,21 @@
         own[t] = mine
         coup[t, yr] = mine
 
-        def share(i, carry):
+        for i in FAR_FIRST[:-1]:
             pltpu.make_async_remote_copy(
                 src_ref=own.at[t], dst_ref=coup.at[t, yr],
                 send_sem=ag_send.at[t], recv_sem=ag_recv.at[t],
                 device_id=(row_peer(i, yr), yc), device_id_type=MESH,
             ).start()
-            return carry
-
-        lax.fori_loop(1, ROWS, share, 0, unroll=True)
 
         @pl.when(second_pair)
         def _():
-            def lend(i, carry):
+            for i in FAR_FIRST:
                 pltpu.make_async_remote_copy(
                     src_ref=own.at[t], dst_ref=coupn.at[t, yr - 16],
                     send_sem=lend_send.at[t], recv_sem=lend_recv.at[t],
                     device_id=(row_peer(i, yr), before if t else after), device_id_type=MESH,
                 ).start()
-                return carry
-
-            lax.fori_loop(0, ROWS, lend, 0, unroll=True)
 
         late()
         whole = coup.at[t, pl.ds(0, ROWS - 1)]
@@ -413,8 +413,8 @@
             pltpu.VMEM((PIX, 128), F32),
             pltpu.VMEM((PIX, 128), F32),
             pltpu.VMEM((4, 128), F32),
-            pltpu.VMEM((2, ROWS, 12, 128), F32),
-            pltpu.VMEM((2, ROWS, 12, 128), F32),
+            pltpu.VMEM((2, ROWS, 10, 128), F32),
+            pltpu.VMEM((2, ROWS, 10, 128), F32),
             pltpu.VMEM((2, 8, 128), F32),
             pltpu.VMEM((2, ROWS, 8, 128), F32),
             pltpu.VMEM((2, 16, 8, 128), F32),

time: 119 us -> 115 us (0.966)
  Pallas kernels: 117 us -> 114 us
    pallas_call x1, Pallas kernels: 112 us -> 109 us  [two_steps(): pl.pallas_call(steps_kernel, out_shape=(jax.ShapeDtypeStruct((4, PIX, 128...]
where the time goes in v2:
time: 115 us
  Pallas kernels  114 us (99%)
  local copies, waits for them, and re-layouts  1.37 us (1%)
    pallas_call x1, Pallas kernels, two_steps(): pl.pallas_call(steps_kernel, out_shape=(jax.ShapeDtypeStruct((4, PIX, 128...  109 us
    pallas_call x1, Pallas kernels, finish(): pl.pallas_call(finish_kernel, grid=(PIX // rows,), out_shape=jax.ShapeDty...  5.05 us

profile of v2, /device:TPU:1, one launch (start us, length us, event | category | flops | bytes accessed | tf_op | source)
XLA Modules:
  0.0 115.2 jit_solution(16346422367797426422)
XLA Ops:
  0.0 0.0 copy-start
  0.0 0.7 copy-done
  0.7 0.0 copy-start.1
  0.7 0.7 copy-done.1
  1.4 108.8 %shard_map.37 = (f32[4,2048,128]{2,1,0:T(8,128)S(1)}, f32[2048,128]{1,0:T(8,128)S(1)}, f32[2048,128]{1,0:T(8,128)S(1)}, f32[256,512]{1,0:T(8,128)S(1)}) custom-call(f32[8192,128]{1,0:T(8,128)} %bitcast.5, s32[2048]{0:T(1024)S(1)} %copy-done, s32[2,4]{1,0:T(2,128)S(1)} %copy-done.1), custom_call_target="tpu_custom_call" | custom-call | tf_op jit(solution)/shard_map/pallas_call | solution.py:394
  110.1 5.0 %shard_map.38 = f32[2048,512]{1,0:T(8,128)} custom-call(f32[4,2048,128]{2,1,0:T(8,128)S(1)} %get-tuple-element.9.y_ref, f32[2048,128]{1,0:T(8,128)S(1)} %get-tuple-element.10.z_ref, f32[2048,128]{1,0:T(8,128)S(1)} %get-tuple-element.11.qn_ref, f32[256,512]{1,0:T(8,128)S(1)} %get-tuple-element.12.turn_ref, s32[2,4]{1,0:T(2,128)S(1)} %copy-done.1), custom_call_target="tpu_custom_call" | custom-call | tf_op jit(solution)/shard_map/pallas_call | solution.py:453
Async XLA Ops:
  0.0 0.7 copy-start
  0.7 0.7 copy-start.1

commit v3 on v2

--- a/solution.py
+++ b/solution.py
@@ -285,45 +285,49 @@
         rot[k, 128:, :128] = down
         rot[k, 128:, 128:] = low
 
+    def square(x):
+        return jnp.sum(x * x, axis=0, keepdims=True)
+
     def turn_second(i):
         x = jnp.concatenate([xt[c, tile(i), :], xt[3, tile(i), :]], axis=1)
         turned = product(x, rot[1])
         yy[3, tile(i), :] = turned[:, 128:]
         yy[2, tile(i), :] = turned[:, :128]
+        return square(turned[:, :128])
 
     def turn_first(i):
         x = jnp.concatenate([xt[a, tile(i), :], xt[b, tile(i), :]], axis=1)
         turned = product(x, rot[0])
         yy[0, tile(i), :] = turned[:, :128]
         yy[1, tile(i), :] = turned[:, 128:]
+        return square(turned)
 
     def turn_own(i, carry):
-        turn_first(i)
-        turn_second(i)
-        return carry
-
-    turn_second(raw)
+        return carry[0] + turn_first(i), carry[1] + turn_second(i)
+
+    square_c = turn_second(raw)
     forward(2 * raw).start()
-    turn_first(raw)
-    lax.fori_loop(0, raw, turn_own, 0)
+    square_ab, square_c = lax.fori_loop(0, raw, turn_own, (turn_first(raw), square_c))
+    diag[0:1, :] = square_ab[:, :128]
+    diag[1:2, :] = square_ab[:, 128:]
+    diag[2:3, :] = square_c
     keep = pltpu.make_async_copy(yy, y_ref, out_sem.at[0])
-    keep.start()
 
     def role_of(slot):
         return jnp.where(slot == a, 0, jnp.where(slot == b, 1, 2))
 
     a2, b2, c2 = (role_of(slot) for slot in roles(pairing_ref[1, yc]))
     gram_p = gram(lambda i: yy[a2, tile(i), :], lambda i: yy[b2, tile(i), :])
-    lows = [squares(lambda i, k=k: yy[k, tile(i), :]) for k in (a2, b2, c2)]
+    lows = [diag[pl.ds(k, 1), :] for k in (a2, b2, c2)]
 
     for k in range(2 * raw):
         forward(k).wait_recv()
 
     def meet(i, block, carry):
-        total, square = carry
+        total, norms = carry
         return (
             total + product_of_rows(yy[c2, tile(i), :], block),
-            square + jnp.sum(block * block, axis=0, keepdims=True),
+            norms + square(block),
         )
 
     def turn_and_meet(i, carry):
@@ -338,7 +342,6 @@
     forward(2 * raw).wait_recv()
     gram_q, last = meet(raw, z[tile(raw), :], met)
     keep_z = pltpu.make_async_copy(z, z_ref, out_sem.at[1])
-    keep_z.start()
     for k in range(raw):
         forward(k).wait_send()
 
@@ -353,6 +356,8 @@
         q[upper, :] = yy[c2, upper, :]
         backward(0).start()
         q[lower, :] = yy[c2, lower, :]
+        keep.start()
+        keep_z.start()
 
     first, second, third = summed(
         1, gram_p, gram_q, (*lows, last), early_second, lambda: backward(1).start()

time: 115 us -> 114 us (level)
    pallas_call x1, Pallas kernels: 109 us -> 107 us  [two_steps(): pl.pallas_call(steps_kernel, out_shape=(jax.ShapeDtypeStruct((4, PIX, 128...]
where the time goes in v3:
time: 114 us
  Pallas kernels  113 us (99%)
  local copies, waits for them, and re-layouts  1.37 us (1%)
    pallas_call x1, Pallas kernels, two_steps(): pl.pallas_call(steps_kernel, out_shape=(jax.ShapeDtypeStruct((4, PIX, 128...  107 us
    pallas_call x1, Pallas kernels, finish(): pl.pallas_call(finish_kernel, grid=(PIX // rows,), out_shape=jax.ShapeDty...  5.05 us

profile of v3, /device:TPU:1, one launch (start us, length us, event | category | flops | bytes accessed | tf_op | source)
XLA Modules:
  0.0 113.9 jit_solution(6746420137039161373)
XLA Ops:
  0.0 0.0 copy-start
  0.0 0.7 copy-done
  0.7 0.0 copy-start.1
  0.7 0.7 copy-done.1
  1.4 107.5 %shard_map.37 = (f32[4,2048,128]{2,1,0:T(8,128)S(1)}, f32[2048,128]{1,0:T(8,128)S(1)}, f32[2048,128]{1,0:T(8,128)S(1)}, f32[256,512]{1,0:T(8,128)S(1)}) custom-call(f32[8192,128]{1,0:T(8,128)} %bitcast.5, s32[2048]{0:T(1024)S(1)} %copy-done, s32[2,4]{1,0:T(2,128)S(1)} %copy-done.1), custom_call_target="tpu_custom_call" | custom-call | tf_op jit(solution)/shard_map/pallas_call | solution.py:399
  108.9 5.0 %shard_map.38 = f32[2048,512]{1,0:T(8,128)} custom-call(f32[4,2048,128]{2,1,0:T(8,128)S(1)} %get-tuple-element.9.y_ref, f32[2048,128]{1,0:T(8,128)S(1)} %get-tuple-element.10.z_ref, f32[2048,128]{1,0:T(8,128)S(1)} %get-tuple-element.11.qn_ref, f32[256,512]{1,0:T(8,128)S(1)} %get-tuple-element.12.turn_ref, s32[2,4]{1,0:T(2,128)S(1)} %copy-done.1), custom_call_target="tpu_custom_call" | custom-call | tf_op jit(solution)/shard_map/pallas_call | solution.py:458
Async XLA Ops:
  0.0 0.7 copy-start
  0.7 0.7 copy-start.1

commit v4 on v3

--- a/solution.py
+++ b/solution.py
@@ -179,11 +179,81 @@
 
         lax.fori_loop(0, PIX // 16, move, 0)
 
+    owns_first = (yr & 1) == 0
+
+    def deal(t, p, cross, diagonals):
+        low = jnp.concatenate(diagonals, axis=0)
+        for k in range(16):
+            parts[t, 2 * k + p, 0:8, :] = cross[8 * k : 8 * k + 8]
+            parts[t, 2 * k + p, 8:10, :] = low
+        odd = (yr + p) & 1
+
+        def give(m):
+            r = row_peer(2 * m + odd, yr)
+            pltpu.make_async_remote_copy(
+                src_ref=parts.at[t, r], dst_ref=arrived.at[t, yr],
+                send_sem=rs_send.at[t], recv_sem=rs_recv.at[t],
+                device_id=(r, yc), device_id_type=MESH,
+            ).start()
+
+        for m in sorted(range(1, 16), key=lambda m: hops(2 * m + 1), reverse=True):
+            give(m)
+
+        @pl.when(odd == 1)
+        def _():
+            give(0)
+
+        @pl.when(odd == 0)
+        def _():
+            arrived[t, yr] = parts[t, yr]
+
+    def own_part(t, p):
+        whole = arrived.at[t, pl.ds(0, ROWS - 1)]
+        pltpu.make_async_copy(whole, whole, rs_recv.at[t]).wait()
+        total = arrived[t, 0]
+        for r in range(1, ROWS):
+            total = total + arrived[t, r]
+        left, right = total[8:9], total[9:10]
+        spot = lax.broadcasted_iota(jnp.int32, (8, 128), 0) + 8 * (yr >> 1)
+        lane = lax.broadcasted_iota(jnp.int32, (8, 128), 1)
+        left = jnp.sum(jnp.where(spot == lane, jnp.broadcast_to(left, (8, 128)), 0.0), axis=1, keepdims=True)
+        mine = total[0:8] / (left + right)
+        own[t] = mine
+        coup[t, p, yr >> 1] = mine
+        for i in FAR_FIRST[:-1]:
+            pltpu.make_async_remote_copy(
+                src_ref=own.at[t], dst_ref=coup.at[t, p, yr >> 1],
+                send_sem=ag_send.at[t], recv_sem=ag_recv.at[2 * t + p],
+                device_id=(row_peer(i, yr), yc), device_id_type=MESH,
+            ).start()
+        if p == 1:
+            for i in FAR_FIRST:
+                pltpu.make_async_remote_copy(
+                    src_ref=own.at[t], dst_ref=coupn.at[t, yr >> 1],
+                    send_sem=lend_send.at[t], recv_sem=lend_recv.at[t],
+                    device_id=(row_peer(i, yr), before if t else after), device_id_type=MESH,
+                ).start()
+
+    def shared(t, p):
+        mine = (yr & 1) == p
+        for count, chosen in ((15, mine), (16, jnp.logical_not(mine))):
+            @pl.when(chosen)
+            def _(count=count):
+                whole = coup.at[t, p, pl.ds(0, count)]
+                pltpu.make_async_copy(whole, whole, ag_recv.at[2 * t + p]).wait()
+
+        return coup[t, p].reshape(128, 128)
+
+    def lent(t):
+        whole = coupn.at[t]
+        pltpu.make_async_copy(whole, whole, lend_recv.at[t]).wait()
+        return coupn[t].reshape(128, 128)
+
     a, b, c = roles(pairing_ref[0, yc])
-    gram_p = None
     for s in range(4):
         if s == 3:
             gram_p = gram(lambda i: flat[a, tile(i), :], lambda i: flat[b, tile(i), :])
+            deal(0, 0, gram_p, (diag[pl.ds(a, 1), :], diag[pl.ds(b, 1), :]))
         whole = recv.at[s, pl.ds(0, ALL - 1)]
         pltpu.make_async_copy(whole, whole, a2a_recv.at[s]).wait()
         for g in range(16):
@@ -192,63 +262,6 @@
         if s < 3:
             place(s)
 
-    def summed(t, first, second, diagonals, early, late):
-        lows = [jnp.concatenate(diagonals[k : k + 2], axis=0) for k in (0, 2)]
-        for r in range(16):
-            parts[t, r, 0:8, :] = first[8 * r : 8 * r + 8]
-            parts[t, 16 + r, 0:8, :] = second[8 * r : 8 * r + 8]
-        for r in range(ROWS):
-            parts[t, r, 8:10, :] = lows[r // 16]
-
-        for i in FAR_FIRST[:-1]:
-            r = row_peer(i, yr)
-            pltpu.make_async_remote_copy(
-                src_ref=parts.at[t, r], dst_ref=arrived.at[t, yr],
-                send_sem=rs_send.at[t], recv_sem=rs_recv.at[t],
-                device_id=(r, yc), device_id_type=MESH,
-            ).start()
-        arrived[t, yr] = parts[t, yr]
-        early()
-        whole = arrived.at[t, pl.ds(0, ROWS - 1)]
-        pltpu.make_async_copy(whole, whole, rs_recv.at[t]).wait()
-        total = arrived[t, 0]
-        for r in range(1, ROWS):
-            total = total + arrived[t, r]
-        second_pair = yr >= 16
-        left, right = total[8:9], total[9:10]
-        spot = lax.broadcasted_iota(jnp.int32, (8, 128), 0) + 8 * (yr & 15)
-        lane = lax.broadcasted_iota(jnp.int32, (8, 128), 1)
-        left = jnp.sum(jnp.where(spot == lane, jnp.broadcast_to(left, (8, 128)), 0.0), axis=1, keepdims=True)
-        mine = total[0:8] / (left + right)
-        own[t] = mine
-        coup[t, yr] = mine
-
-        for i in FAR_FIRST[:-1]:
-            pltpu.make_async_remote_copy(
-                src_ref=own.at[t], dst_ref=coup.at[t, yr],
-                send_sem=ag_send.at[t], recv_sem=ag_recv.at[t],
-                device_id=(row_peer(i, yr), yc), device_id_type=MESH,
-            ).start()
-
-        @pl.when(second_pair)
-        def _():
-            for i in FAR_FIRST:
-                pltpu.make_async_remote_copy(
-                    src_ref=own.at[t], dst_ref=coupn.at[t, yr - 16],
-                    send_sem=lend_send.at[t], recv_sem=lend_recv.at[t],
-                    device_id=(row_peer(i, yr), before if t else after), device_id_type=MESH,
-                ).start()
-
-        late()
-        whole = coup.at[t, pl.ds(0, ROWS - 1)]
-        pltpu.make_async_copy(whole, whole, ag_recv.at[t]).wait()
-        whole = coupn.at[t]
-        pltpu.make_async_copy(whole, whole, lend_recv.at[t]).wait()
-        both = coup[t].reshape(256, 128)
-        return both[:128], both[128:], coupn[t].reshape(128, 128)
-
-    half = PIX // 2
-    upper, lower = pl.ds(0, half), pl.ds(half, half)
     raw = TILES - 1
 
     def forward(k):
@@ -264,22 +277,26 @@
     forward(0).start()
     gram_q = gram(lambda i: flat[c, tile(i), :], lambda i: flat[3, tile(i), :])
 
-    def early_first():
-        for k in range(1, raw):
-            q[pl.ds(k * TILE, TILE), :] = xt[c, pl.ds(k * TILE, TILE), :]
-            forward(k).start()
-        place(3)
-
-    def late_first():
-        for k in range(raw, 2 * raw):
-            forward(k).start()
-
-    first, second, third = summed(
-        0, gram_p, gram_q,
-        (diag[pl.ds(a, 1), :], diag[pl.ds(b, 1), :], diag[pl.ds(c, 1), :], diag[3:4, :]),
-        early_first, late_first,
-    )
-    for k, (top, cross, down, low) in enumerate(rotations((first, second, third), state, weight)):
+    deal(0, 1, gram_q, (diag[pl.ds(c, 1), :], diag[3:4, :]))
+
+    @pl.when(owns_first)
+    def _():
+        own_part(0, 0)
+
+    for k in range(1, raw):
+        q[pl.ds(k * TILE, TILE), :] = xt[c, pl.ds(k * TILE, TILE), :]
+        forward(k).start()
+    place(3)
+
+    @pl.when(jnp.logical_not(owns_first))
+    def _():
+        own_part(0, 1)
+
+    for k in range(raw, 2 * raw):
+        forward(k).start()
+
+    def keep_rotation(k, parts_of):
+        top, cross, down, low = parts_of
         rot[k, :128, :128] = top
         rot[k, :128, 128:] = cross
         rot[k, 128:, :128] = down
@@ -302,12 +319,15 @@
         yy[1, tile(i), :] = turned[:, 128:]
         return square(turned)
 
-    def turn_own(i, carry):
-        return carry[0] + turn_first(i), carry[1] + turn_second(i)
-
+    keep_rotation(0, rotations((shared(0, 0),), state, weight)[0])
+    square_ab = lax.fori_loop(
+        0, TILES, lambda i, carry: carry + turn_first(i), jnp.zeros((1, 256), F32)
+    )
+    for k, turn in enumerate(rotations((shared(0, 1), lent(0)), state, weight)):
+        keep_rotation(1 + k, turn)
     square_c = turn_second(raw)
     forward(2 * raw).start()
-    square_ab, square_c = lax.fori_loop(0, raw, turn_own, (turn_first(raw), square_c))
+    square_c = lax.fori_loop(0, raw, lambda i, carry: carry + turn_second(i), square_c)
     diag[0:1, :] = square_ab[:, :128]
     diag[1:2, :] = square_ab[:, 128:]
     diag[2:3, :] = square_c
@@ -318,7 +338,7 @@
 
     a2, b2, c2 = (role_of(slot) for slot in roles(pairing_ref[1, yc]))
     gram_p = gram(lambda i: yy[a2, tile(i), :], lambda i: yy[b2, tile(i), :])
-    lows = [diag[pl.ds(k, 1), :] for k in (a2, b2, c2)]
+    deal(1, 0, gram_p, (diag[pl.ds(a2, 1), :], diag[pl.ds(b2, 1), :]))
 
     for k in range(2 * raw):
         forward(k).wait_recv()
@@ -346,23 +366,33 @@
         forward(k).wait_send()
 
     def backward(k):
-        part = (upper, lower)[k]
+        part = tile(k)
         return pltpu.make_async_remote_copy(
             src_ref=q.at[part], dst_ref=qn_ref.at[part], send_sem=q_send.at[k], recv_sem=q_recv.at[k],
             device_id=(yr, before), device_id_type=MESH,
         )
 
-    def early_second():
-        q[upper, :] = yy[c2, upper, :]
-        backward(0).start()
-        q[lower, :] = yy[c2, lower, :]
-        keep.start()
-        keep_z.start()
-
-    first, second, third = summed(
-        1, gram_p, gram_q, (*lows, last), early_second, lambda: backward(1).start()
-    )
-    turns = rotations((first, second, third), state, weight)
+    deal(1, 1, gram_q, (diag[pl.ds(c2, 1), :], last))
+    for k in range(TILES):
+        q[tile(k), :] = yy[c2, tile(k), :]
+    backward(0).start()
+
+    @pl.when(owns_first)
+    def _():
+        own_part(1, 0)
+        backward(1).start()
+
+    @pl.when(jnp.logical_not(owns_first))
+    def _():
+        backward(1).start()
+        own_part(1, 1)
+
+    for k in range(2, TILES):
+        backward(k).start()
+    keep.start()
+    keep_z.start()
+    turns = rotations((shared(1, 0),), state, weight)
+    turns += rotations((shared(1, 1), lent(1)), state, weight)
     turn_ref[:128, 0:128] = turns[0][0]
     turn_ref[:128, 128:256] = turns[0][1]
     turn_ref[128:, 0:128] = turns[0][2]
@@ -376,7 +406,7 @@
     keep_z.wait()
     for k in range(raw, 2 * raw + 1):
         forward(k).wait_send()
-    for k in range(2):
+    for k in range(TILES):
         backward(k).wait()
     for s in range(4):
         whole = recv.at[s, pl.ds(0, ALL - 1)]
@@ -384,13 +414,13 @@
     for t in range(2):
         whole = arrived.at[t, pl.ds(0, ROWS - 1)]
         pltpu.make_async_copy(whole, whole, rs_send.at[t]).wait()
-        whole = coup.at[t, pl.ds(0, ROWS - 1)]
+        whole = flat.at[0, pl.ds(0, 8 * (ROWS - 1))]
         pltpu.make_async_copy(whole, whole, ag_send.at[t]).wait()
 
-    @pl.when(yr >= 16)
+    @pl.when(jnp.logical_not(owns_first))
     def _():
         for t in range(2):
-            whole = coup.at[t]
+            whole = flat.at[0, pl.ds(0, 8 * ROWS)]
             pltpu.make_async_copy(whole, whole, lend_send.at[t]).wait()
 
 
@@ -421,13 +451,13 @@
             pltpu.VMEM((2, ROWS, 10, 128), F32),
             pltpu.VMEM((2, ROWS, 10, 128), F32),
             pltpu.VMEM((2, 8, 128), F32),
-            pltpu.VMEM((2, ROWS, 8, 128), F32),
+            pltpu.VMEM((2, 2, 16, 8, 128), F32),
             pltpu.VMEM((2, 16, 8, 128), F32),
             pltpu.VMEM((3, 256, 256), F32),
             pltpu.VMEM((6, 256, 128), F32),
             pltpu.VMEM((6, 128, 128), F32),
-            dma((8,)), dma((2,)), dma, dma((4,)), dma((2,)), dma((2,)), dma((2,)), dma((2,)), dma((2,)), dma((2,)),
-            dma((2 * TILES - 1,)), dma((2 * TILES - 1,)), dma((2,)), dma((2,)),
+            dma((8,)), dma((2,)), dma, dma((4,)), dma((2,)), dma((2,)), dma((2,)), dma((4,)), dma((2,)), dma((2,)),
+            dma((2 * TILES - 1,)), dma((2 * TILES - 1,)), dma((TILES,)), dma((TILES,)),
         ],
         compiler_params=pltpu.CompilerParams(
             collective_id=0, has_side_effects=True, vmem_limit_bytes=VMEM

time: 114 us -> 112 us (0.982)
  Pallas kernels: 113 us -> 110 us
    pallas_call x1, Pallas kernels: 107 us -> 105 us  [two_steps(): pl.pallas_call(steps_kernel, out_shape=(jax.ShapeDtypeStruct((4, PIX, 128...]
where the time goes in v4:
time: 112 us
  Pallas kernels  110 us (98%)
  local copies, waits for them, and re-layouts  1.37 us (1%)
    pallas_call x1, Pallas kernels, two_steps(): pl.pallas_call(steps_kernel, out_shape=(jax.ShapeDtypeStruct((4, PIX, 128...  105 us
    pallas_call x1, Pallas kernels, finish(): pl.pallas_call(finish_kernel, grid=(PIX // rows,), out_shape=jax.ShapeDty...  5.04 us

profile of v4, /device:TPU:1, one launch (start us, length us, event | category | flops | bytes accessed | tf_op | source)
XLA Modules:
  0.0 111.7 jit_solution(3441115101014586896)
XLA Ops:
  0.0 0.0 copy-start
  0.0 0.7 copy-done
  0.7 0.0 copy-start.1
  0.7 0.7 copy-done.1
  1.4 105.3 %shard_map.37 = (f32[4,2048,128]{2,1,0:T(8,128)S(1)}, f32[2048,128]{1,0:T(8,128)S(1)}, f32[2048,128]{1,0:T(8,128)S(1)}, f32[256,512]{1,0:T(8,128)S(1)}) custom-call(f32[8192,128]{1,0:T(8,128)} %bitcast.5, s32[2048]{0:T(1024)S(1)} %copy-done, s32[2,4]{1,0:T(2,128)S(1)} %copy-done.1), custom_call_target="tpu_custom_call" | custom-call | tf_op jit(solution)/shard_map/pallas_call | solution.py:429
  106.7 5.0 %shard_map.38 = f32[2048,512]{1,0:T(8,128)} custom-call(f32[4,2048,128]{2,1,0:T(8,128)S(1)} %get-tuple-element.9.y_ref, f32[2048,128]{1,0:T(8,128)S(1)} %get-tuple-element.10.z_ref, f32[2048,128]{1,0:T(8,128)S(1)} %get-tuple-element.11.qn_ref, f32[256,512]{1,0:T(8,128)S(1)} %get-tuple-element.12.turn_ref, s32[2,4]{1,0:T(2,128)S(1)} %copy-done.1), custom_call_target="tpu_custom_call" | custom-call | tf_op jit(solution)/shard_map/pallas_call | solution.py:488
Async XLA Ops:
  0.0 0.7 copy-start
  0.7 0.7 copy-start.1

commit v5 on v4

--- a/solution.py
+++ b/solution.py
@@ -161,7 +161,7 @@
         def add(i, carry):
             return carry + product_of_rows(left(i), right(i))
 
-        return lax.fori_loop(0, TILES, add, jnp.zeros((128, 128), F32))
+        return lax.fori_loop(0, TILES, add, jnp.zeros((128, 128), F32), unroll=True)
 
     def squares(block):
         def add(i, carry):
@@ -249,19 +249,6 @@
         pltpu.make_async_copy(whole, whole, lend_recv.at[t]).wait()
         return coupn[t].reshape(128, 128)
 
-    a, b, c = roles(pairing_ref[0, yc])
-    for s in range(4):
-        if s == 3:
-            gram_p = gram(lambda i: flat[a, tile(i), :], lambda i: flat[b, tile(i), :])
-            deal(0, 0, gram_p, (diag[pl.ds(a, 1), :], diag[pl.ds(b, 1), :]))
-        whole = recv.at[s, pl.ds(0, ALL - 1)]
-        pltpu.make_async_copy(whole, whole, a2a_recv.at[s]).wait()
-        for g in range(16):
-            flat[s, pl.ds(g * 128, 128), :] = recv[s, :, g, :].T
-        diag[pl.ds(s, 1), :] = squares(lambda i, s=s: flat[s, tile(i), :])
-        if s < 3:
-            place(s)
-
     raw = TILES - 1
 
     def forward(k):
@@ -273,11 +260,34 @@
             device_id=(yr, after), device_id_type=MESH,
         )
 
+    def square(x):
+        return jnp.sum(x * x, axis=0, keepdims=True)
+
+    a, b, c = roles(pairing_ref[0, yc])
+    for s in range(4):
+        if s == 3:
+            gram_p = gram(lambda i: flat[a, tile(i), :], lambda i: flat[b, tile(i), :])
+            deal(0, 0, gram_p, (diag[pl.ds(a, 1), :], diag[pl.ds(b, 1), :]))
+        whole = recv.at[s, pl.ds(0, ALL - 1)]
+        pltpu.make_async_copy(whole, whole, a2a_recv.at[s]).wait()
+        if s < 3:
+            for g in range(16):
+                flat[s, pl.ds(g * 128, 128), :] = recv[s, :, g, :].T
+            diag[pl.ds(s, 1), :] = squares(lambda i, s=s: flat[s, tile(i), :])
+            place(s)
+
     q[pl.ds(0, TILE), :] = xt[c, pl.ds(0, TILE), :]
     forward(0).start()
-    gram_q = gram(lambda i: flat[c, tile(i), :], lambda i: flat[3, tile(i), :])
-
-    deal(0, 1, gram_q, (diag[pl.ds(c, 1), :], diag[3:4, :]))
+    gram_q = jnp.zeros((128, 128), F32)
+    square_3 = jnp.zeros((1, 128), F32)
+    span = TILE // 128
+    for k in range(TILES):
+        block = jnp.concatenate([recv[3, :, span * k + g, :].T for g in range(span)], axis=0)
+        flat[3, tile(k), :] = block
+        gram_q = gram_q + product_of_rows(flat[c, tile(k), :], block)
+        square_3 = square_3 + square(block)
+
+    deal(0, 1, gram_q, (diag[pl.ds(c, 1), :], square_3))
 
     @pl.when(owns_first)
     def _():
@@ -301,9 +311,6 @@
         rot[k, :128, 128:] = cross
         rot[k, 128:, :128] = down
         rot[k, 128:, 128:] = low
-
-    def square(x):
-        return jnp.sum(x * x, axis=0, keepdims=True)
 
     def turn_second(i):
         x = jnp.concatenate([xt[c, tile(i), :], xt[3, tile(i), :]], axis=1)
@@ -327,7 +334,7 @@
         keep_rotation(1 + k, turn)
     square_c = turn_second(raw)
     forward(2 * raw).start()
-    square_c = lax.fori_loop(0, raw, lambda i, carry: carry + turn_second(i), square_c)
+    square_c = lax.fori_loop(0, raw, lambda i, carry: carry + turn_second(i), square_c, unroll=True)
     diag[0:1, :] = square_ab[:, :128]
     diag[1:2, :] = square_ab[:, 128:]
     diag[2:3, :] = square_c
@@ -357,7 +364,7 @@
         return meet(i, block, carry)
 
     met = lax.fori_loop(
-        0, raw, turn_and_meet, (jnp.zeros((128, 128), F32), jnp.zeros((1, 128), F32))
+        0, raw, turn_and_meet, (jnp.zeros((128, 128), F32), jnp.zeros((1, 128), F32)), unroll=True
     )
     forward(2 * raw).wait_recv()
     gram_q, last = meet(raw, z[tile(raw), :], met)

time: 112 us -> 111 us (level)
    pallas_call x1, Pallas kernels: 105 us -> 104 us  [two_steps(): pl.pallas_call(steps_kernel, out_shape=(jax.ShapeDtypeStruct((4, PIX, 128...]
where the time goes in v5:
time: 111 us
  Pallas kernels  109 us (98%)
  local copies, waits for them, and re-layouts  1.37 us (1%)
    pallas_call x1, Pallas kernels, two_steps(): pl.pallas_call(steps_kernel, out_shape=(jax.ShapeDtypeStruct((4, PIX, 128...  104 us
    pallas_call x1, Pallas kernels, finish(): pl.pallas_call(finish_kernel, grid=(PIX // rows,), out_shape=jax.ShapeDty...  5.05 us

profile of v5, /device:TPU:1, one launch (start us, length us, event | category | flops | bytes accessed | tf_op | source)
XLA Modules:
  0.0 110.6 jit_solution(968857626781433867)
XLA Ops:
  0.0 0.0 copy-start
  0.0 0.7 copy-done
  0.7 0.0 copy-start.1
  0.7 0.7 copy-done.1
  1.4 104.2 %shard_map.37 = (f32[4,2048,128]{2,1,0:T(8,128)S(1)}, f32[2048,128]{1,0:T(8,128)S(1)}, f32[2048,128]{1,0:T(8,128)S(1)}, f32[256,512]{1,0:T(8,128)S(1)}) custom-call(f32[8192,128]{1,0:T(8,128)} %bitcast.5, s32[2048]{0:T(1024)S(1)} %copy-done, s32[2,4]{1,0:T(2,128)S(1)} %copy-done.1), custom_call_target="tpu_custom_call" | custom-call | tf_op jit(solution)/shard_map/pallas_call | solution.py:436
  105.6 5.0 %shard_map.38 = f32[2048,512]{1,0:T(8,128)} custom-call(f32[4,2048,128]{2,1,0:T(8,128)S(1)} %get-tuple-element.9.y_ref, f32[2048,128]{1,0:T(8,128)S(1)} %get-tuple-element.10.z_ref, f32[2048,128]{1,0:T(8,128)S(1)} %get-tuple-element.11.qn_ref, f32[256,512]{1,0:T(8,128)S(1)} %get-tuple-element.12.turn_ref, s32[2,4]{1,0:T(2,128)S(1)} %copy-done.1), custom_call_target="tpu_custom_call" | custom-call | tf_op jit(solution)/shard_map/pallas_call | solution.py:495
Async XLA Ops:
  0.0 0.7 copy-start
  0.7 0.7 copy-start.1

commit v6 on v5

--- a/solution.py
+++ b/solution.py
@@ -37,6 +37,11 @@
     return (y << 3) + ((x >> 1) << 2) + z, ((x & 1) << 1) + ((yc + i) & 1)
 
 
+def distance(i):
+    first, second, third = i >> 1 & 3, i >> 3 & 3, i >> 5
+    return sum((0, 1, 2, 1)[k & 3] for k in (first + second, first, first + third + 2 * second))
+
+
 def row_peer(i, yr):
     y = ((yr >> 3) + (i >> 2)) & 3
     x = ((yr >> 2) + (i >> 4)) & 1
@@ -126,11 +131,8 @@
         load(s).start()
         load(4 + s).start()
 
-    def greet(i, carry):
+    for i in sorted(range(1, ALL), key=distance, reverse=True):
         pl.semaphore_signal(barrier, inc=1, device_id=any_peer(i, yr, yc), device_id_type=MESH)
-        return carry
-
-    lax.fori_loop(1, ALL, greet, 0, unroll=9)
     for s in range(4):
         load(s).wait()
         load(4 + s).wait()
@@ -328,7 +330,7 @@
 
     keep_rotation(0, rotations((shared(0, 0),), state, weight)[0])
     square_ab = lax.fori_loop(
-        0, TILES, lambda i, carry: carry + turn_first(i), jnp.zeros((1, 256), F32)
+        0, TILES, lambda i, carry: carry + turn_first(i), jnp.zeros((1, 256), F32), unroll=True
     )
     for k, turn in enumerate(rotations((shared(0, 1), lent(0)), state, weight)):
         keep_rotation(1 + k, turn)

time: 111 us -> 110 us (level)
    pallas_call x1, Pallas kernels: 104 us -> 103 us  [two_steps(): pl.pallas_call(steps_kernel, out_shape=(jax.ShapeDtypeStruct((4, PIX, 128...]
where the time goes in v6:
time: 110 us; the launch traced here: 109 us
  Pallas kernels  108 us (98%)
  local copies, waits for them, and re-layouts  1.37 us (1%)
    pallas_call x1, Pallas kernels, two_steps(): pl.pallas_call(steps_kernel, out_shape=(jax.ShapeDtypeStruct((4, PIX, 128...  103 us
    pallas_call x1, Pallas kernels, finish(): pl.pallas_call(finish_kernel, grid=(PIX // rows,), out_shape=jax.ShapeDty...  5.05 us

profile of v6, /device:TPU:1, one launch (start us, length us, event | category | flops | bytes accessed | tf_op | source)
XLA Modules:
  0.0 109.5 jit_solution(2734023469140567381)
XLA Ops:
  0.0 0.0 copy-start
  0.0 0.7 copy-done
  0.7 0.0 copy-start.1
  0.7 0.7 copy-done.1
  1.4 103.0 %shard_map.37 = (f32[4,2048,128]{2,1,0:T(8,128)S(1)}, f32[2048,128]{1,0:T(8,128)S(1)}, f32[2048,128]{1,0:T(8,128)S(1)}, f32[256,512]{1,0:T(8,128)S(1)}) custom-call(f32[8192,128]{1,0:T(8,128)} %bitcast.5, s32[2048]{0:T(1024)S(1)} %copy-done, s32[2,4]{1,0:T(2,128)S(1)} %copy-done.1), custom_call_target="tpu_custom_call" | custom-call | tf_op jit(solution)/shard_map/pallas_call | solution.py:438
  104.4 5.0 %shard_map.38 = f32[2048,512]{1,0:T(8,128)} custom-call(f32[4,2048,128]{2,1,0:T(8,128)S(1)} %get-tuple-element.9.y_ref, f32[2048,128]{1,0:T(8,128)S(1)} %get-tuple-element.10.z_ref, f32[2048,128]{1,0:T(8,128)S(1)} %get-tuple-element.11.qn_ref, f32[256,512]{1,0:T(8,128)S(1)} %get-tuple-element.12.turn_ref, s32[2,4]{1,0:T(2,128)S(1)} %copy-done.1), custom_call_target="tpu_custom_call" | custom-call | tf_op jit(solution)/shard_map/pallas_call | solution.py:497
Async XLA Ops:
  0.0 0.7 copy-start
  0.7 0.7 copy-start.1

commit v7 on v6

--- a/solution.py
+++ b/solution.py
@@ -156,7 +156,7 @@
             ).start()
             return carry
 
-        lax.fori_loop(1, ALL, scatter, 0)
+        lax.fori_loop(1, ALL, scatter, 0, unroll=4)
         recv[s, me] = send[((yc & 1) << 2) + s, yc >> 1, yr]
 
     def gram(left, right):

time: 110 us -> 110 us (level)
  no operation moved by 1% of the time
where the time goes in v7:
time: 110 us; the launch traced here: 109 us
  Pallas kernels  108 us (98%)
  local copies, waits for them, and re-layouts  1.37 us (1%)
    pallas_call x1, Pallas kernels, two_steps(): pl.pallas_call(steps_kernel, out_shape=(jax.ShapeDtypeStruct((4, PIX, 128...  103 us
    pallas_call x1, Pallas kernels, finish(): pl.pallas_call(finish_kernel, grid=(PIX // rows,), out_shape=jax.ShapeDty...  5.05 us

profile of v7, /device:TPU:1, one launch (start us, length us, event | category | flops | bytes accessed | tf_op | source)
XLA Modules:
  0.0 109.5 jit_solution(2209523194108630398)
XLA Ops:
  0.0 0.0 copy-start
  0.0 0.7 copy-done
  0.7 0.0 copy-start.1
  0.7 0.7 copy-done.1
  1.4 103.0 %shard_map.37 = (f32[4,2048,128]{2,1,0:T(8,128)S(1)}, f32[2048,128]{1,0:T(8,128)S(1)}, f32[2048,128]{1,0:T(8,128)S(1)}, f32[256,512]{1,0:T(8,128)S(1)}) custom-call(f32[8192,128]{1,0:T(8,128)} %bitcast.5, s32[2048]{0:T(1024)S(1)} %copy-done, s32[2,4]{1,0:T(2,128)S(1)} %copy-done.1), custom_call_target="tpu_custom_call" | custom-call | tf_op jit(solution)/shard_map/pallas_call | solution.py:438
  104.4 5.0 %shard_map.38 = f32[2048,512]{1,0:T(8,128)} custom-call(f32[4,2048,128]{2,1,0:T(8,128)S(1)} %get-tuple-element.9.y_ref, f32[2048,128]{1,0:T(8,128)S(1)} %get-tuple-element.10.z_ref, f32[2048,128]{1,0:T(8,128)S(1)} %get-tuple-element.11.qn_ref, f32[256,512]{1,0:T(8,128)S(1)} %get-tuple-element.12.turn_ref, s32[2,4]{1,0:T(2,128)S(1)} %copy-done.1), custom_call_target="tpu_custom_call" | custom-call | tf_op jit(solution)/shard_map/pallas_call | solution.py:497
Async XLA Ops:
  0.0 0.7 copy-start
  0.7 0.7 copy-start.1
